TPU v7x, 32 devices: a whole 2x2x4 slice. The times are simulated.
32 devices in a mesh: dp: 8 (over y, x, core), seq: 4 (over z).
Axes of the slice: x: 2, y: 2, z: 4, core: 2. Of those that a mesh axis runs over, the one named last changes fastest.
Arguments:
- tokens: bfloat16 [8, 512, 6, 768], P('dp', 'seq'), may hold values from -6 to 6
- kind: int32 [8], P('dp'), may hold values from 0 to 1, as said below
- ln1_gain: float32 [768], replicated, may hold values from 0.1 to 1.9
- w_in: bfloat16 [768, 2304], replicated, may hold values from -0.21875 to 0.21875
- short_taps: float32 [3, 2304], replicated, may hold values from -3 to 3
- cond_taps: float32 [3, 768], replicated, may hold values from -3 to 3
- w_cond: bfloat16 [768, 768], replicated, may hold values from -0.21875 to 0.21875
- cond_bias: float32 [768], replicated, may hold values from -3 to 3
- w_out: bfloat16 [768, 768], replicated, may hold values from -0.21875 to 0.21875
- ln2_gain: float32 [768], replicated, may hold values from 0.1 to 1.9
- w_gate: bfloat16 [768, 3072], replicated, may hold values from -0.21875 to 0.21875
- w_up: bfloat16 [768, 3072], replicated, may hold values from -0.21875 to 0.21875
- w_down: bfloat16 [3072, 768], replicated, may hold values from -0.109375 to 0.109375
- cotangent: bfloat16 [8, 512, 6, 768], P('dp', 'seq'), may hold values from -6 to 6
Outputs:
- layer_out: bfloat16 [8, 512, 6, 768], P('dp', 'seq')
- grad_tokens: bfloat16 [8, 512, 6, 768], P('dp', 'seq')
- grad_ln1: float32 [768], P('seq')
- grad_w_in: float32 [768, 2304], P('seq')
- grad_short_taps: float32 [3, 2304], P(None, 'seq')
- grad_cond_taps: float32 [3, 768], P(None, 'seq')
- grad_w_cond: float32 [768, 768], P('seq')
- grad_cond_bias: float32 [768], P('seq')
- grad_w_out: float32 [768, 768], P('seq')
- grad_ln2: float32 [768], P('seq')
- grad_gate: float32 [768, 3072], P('seq')
- grad_up: float32 [768, 3072], P('seq')
- grad_down: float32 [3072, 768], P('seq')
Inputs may be any that keep to these rules, and one draw needn't show every extreme that they name: Exactly 4 groups have kind 1.
All inputs are finite; a program needn't handle non-finite values.
Results may differ from a plain program's by a relative error of at most 0.017.
Values may be sent and summed in bfloat16 or wider, within the bound.
A program may use at most 256 MiB of HBM per device.

v0:
```python
import math
import jax
import jax.numpy as jnp
from jax import lax
from jax.sharding import PartitionSpec as P

highest = lax.Precision.HIGHEST
epsilon = 1e-05


def from_behind(value, axis, by):
    peers = lax.axis_size(axis)
    pairs = [(i, i + by) for i in range(peers) if 0 <= i + by < peers]
    return lax.ppermute(value, axis, pairs)


def norm_rows(values, scale_gain):
    row_mean = jnp.mean(values, axis=-1, keepdims=True)
    centered = values - row_mean
    scale_inv = lax.rsqrt(jnp.mean(centered * centered, axis=-1, keepdims=True) + epsilon)
    normed = centered * scale_inv
    return (normed * scale_gain, normed, scale_inv)


def norm_back(grad_out, normed, scale_inv, scale_gain):
    grad_gain = jnp.sum(grad_out * normed, axis=0)
    grad_normed = grad_out * scale_gain
    inner_mean = jnp.mean(grad_normed, axis=-1, keepdims=True)
    inner_cross = jnp.mean(grad_normed * normed, axis=-1, keepdims=True)
    return (scale_inv * (grad_normed - inner_mean - normed * inner_cross), grad_gain)


def wave_tables(freq_ids, time_ids, span_len):
    fold_freq = freq_ids[:, None] % span_len
    fold_time = time_ids[None, :] % span_len
    same_block = (freq_ids[:, None] // span_len == time_ids[None, :] // span_len).astype(
        jnp.float32
    )
    phase_index = fold_freq * fold_time % span_len
    phase_angle = phase_index.astype(jnp.float32) * (2.0 * math.pi) / span_len.astype(jnp.float32)
    return (jnp.cos(phase_angle) * same_block, jnp.sin(phase_angle) * same_block)


def conv_forward(extended, taps):
    return taps[0] * extended[2:] + taps[1] * extended[1:-1] + taps[2] * extended[:-2]


def conv_backward(grad_out, extended, taps, long_flag):
    count_rows = grad_out.shape[0]
    zero_pad = jnp.zeros((2,) + grad_out.shape[1:], jnp.float32)
    padded = jnp.concatenate([grad_out, zero_pad], axis=0)
    grad_local = (
        taps[0] * padded[:count_rows] + taps[1] * padded[1 : count_rows + 1] + taps[2] * padded[2:]
    )
    grad_rim = (
        jnp.stack([taps[2] * grad_out[0], taps[1] * grad_out[0] + taps[2] * grad_out[1]])
        * long_flag
    )
    grad_taps = jnp.stack(
        [
            jnp.sum(grad_out * extended[2:], axis=(0, 1)),
            jnp.sum(grad_out * extended[1:-1], axis=(0, 1)),
            jnp.sum(grad_out * extended[:-2], axis=(0, 1)),
        ]
    )
    return (grad_local, grad_rim, grad_taps)


def on_device(
    tokens,
    kind,
    ln1_gain,
    w_in,
    short_taps,
    cond_taps,
    w_cond,
    cond_bias,
    w_out,
    ln2_gain,
    w_gate,
    w_up,
    w_down,
    cotangent,
):
    piece_rows = tokens.shape[1]
    slot_count = tokens.shape[2]
    model_width = tokens.shape[3]
    flat_rows = piece_rows * slot_count
    seq_count = lax.axis_size("seq")
    seq_rank = lax.axis_index("seq")
    is_long = kind[0]
    long_flag = is_long.astype(jnp.float32)
    span_len = jnp.where(is_long == 1, piece_rows * seq_count, piece_rows).astype(jnp.int32)
    span_float = span_len.astype(jnp.float32)
    freq_ids = seq_rank * piece_rows + jnp.arange(piece_rows, dtype=jnp.int32)
    token_rows = tokens.reshape(flat_rows, model_width).astype(jnp.float32)
    normed_one, unit_one, inv_one = norm_rows(token_rows, ln1_gain)
    normed_one_low = normed_one.astype(jnp.bfloat16)
    projected = jnp.dot(normed_one_low, w_in, preferred_element_type=jnp.float32)
    proj_low = projected.astype(jnp.bfloat16).reshape(piece_rows, slot_count, 3 * model_width)
    proj_f = proj_low.astype(jnp.float32)
    rim_proj = from_behind(proj_low[piece_rows - 2 :], "seq", 1).astype(jnp.float32) * long_flag
    extended_proj = jnp.concatenate([rim_proj, proj_f], axis=0)
    conv_out = conv_forward(extended_proj, short_taps)
    query_conv = conv_out[:, :, :model_width]
    key_conv = conv_out[:, :, model_width : 2 * model_width]
    value_low = conv_out[:, :, 2 * model_width :].astype(jnp.bfloat16)
    value_f = value_low.astype(jnp.float32)
    rim_value = from_behind(value_low[piece_rows - 2 :], "seq", 1).astype(jnp.float32) * long_flag
    extended_value = jnp.concatenate([rim_value, value_f], axis=0)
    cond_low = conv_forward(extended_value, cond_taps).astype(jnp.bfloat16)
    signal_low = (key_conv * value_f).astype(jnp.bfloat16)
    sig_piece = lax.all_gather(signal_low, "seq", axis=0, tiled=True).astype(jnp.float32)
    cond_piece = lax.all_gather(cond_low, "seq", axis=0, tiled=True).astype(jnp.float32)
    time_ids = jnp.arange(sig_piece.shape[0], dtype=jnp.int32)
    cos_table, sin_table = wave_tables(freq_ids, time_ids, span_len)
    sig_cos = jnp.einsum("ft,tsd->fsd", cos_table, sig_piece, precision=highest)
    sig_sin = jnp.einsum("ft,tsd->fsd", sin_table, sig_piece, precision=highest)
    cond_cos = jnp.einsum("ft,tsd->fsd", cos_table, cond_piece, precision=highest)
    cond_sin = jnp.einsum("ft,tsd->fsd", sin_table, cond_piece, precision=highest)
    power_spec = (cond_cos * cond_cos + cond_sin * cond_sin) / span_float
    features_low = jnp.log1p(power_spec).astype(jnp.bfloat16).reshape(flat_rows, model_width)
    pre_tanh = jnp.dot(features_low, w_cond, preferred_element_type=jnp.float32) + cond_bias
    tanh_value = jnp.tanh(pre_tanh).reshape(piece_rows, slot_count, model_width)
    spectral_gain = 1.0 + tanh_value
    gained_cos = spectral_gain * sig_cos
    gained_sin = spectral_gain * sig_sin
    time_ids = jnp.arange(piece_rows * lax.axis_size("seq"), dtype=jnp.int32)
    cos_table, sin_table = wave_tables(freq_ids, time_ids, span_len)
    term = jnp.einsum("ft,fsd->tsd", cos_table, gained_cos, precision=highest) + jnp.einsum(
        "ft,fsd->tsd", sin_table, gained_sin, precision=highest
    )
    filtered = lax.psum_scatter(
        (term / span_float).astype(jnp.bfloat16), "seq", scatter_dimension=0, tiled=True
    ).astype(jnp.float32)
    mixed_low = (query_conv * filtered).astype(jnp.bfloat16).reshape(flat_rows, model_width)
    hidden_one = token_rows + jnp.dot(mixed_low, w_out, preferred_element_type=jnp.float32)
    normed_two, unit_two, inv_two = norm_rows(hidden_one, ln2_gain)
    normed_two_low = normed_two.astype(jnp.bfloat16)
    gate_pre = jnp.dot(normed_two_low, w_gate, preferred_element_type=jnp.float32)
    up_proj = jnp.dot(normed_two_low, w_up, preferred_element_type=jnp.float32)
    gate_sig = jax.nn.sigmoid(gate_pre)
    gate_act = gate_pre * gate_sig
    hidden_act = (gate_act * up_proj).astype(jnp.bfloat16)
    layer_rows = hidden_one + jnp.dot(hidden_act, w_down, preferred_element_type=jnp.float32)
    layer_out = layer_rows.astype(jnp.bfloat16).reshape(tokens.shape)
    cot_rows = cotangent.reshape(flat_rows, model_width)
    grad_down = jnp.einsum("nf,nd->fd", hidden_act, cot_rows, preferred_element_type=jnp.float32)
    grad_act = jnp.einsum("nd,fd->nf", cot_rows, w_down, preferred_element_type=jnp.float32)
    grad_gate_pre = (grad_act * up_proj * gate_sig * (1.0 + gate_pre * (1.0 - gate_sig))).astype(
        jnp.bfloat16
    )
    grad_up_proj = (grad_act * gate_act).astype(jnp.bfloat16)
    grad_gate = jnp.einsum(
        "nd,nf->df", normed_two_low, grad_gate_pre, preferred_element_type=jnp.float32
    )
    grad_up = jnp.einsum(
        "nd,nf->df", normed_two_low, grad_up_proj, preferred_element_type=jnp.float32
    )
    grad_normed_two = jnp.einsum(
        "nf,df->nd", grad_gate_pre, w_gate, preferred_element_type=jnp.float32
    ) + jnp.einsum("nf,df->nd", grad_up_proj, w_up, preferred_element_type=jnp.float32)
    grad_hidden_part, grad_ln2 = norm_back(grad_normed_two, unit_two, inv_two, ln2_gain)
    grad_hidden = cot_rows.astype(jnp.float32) + grad_hidden_part
    grad_mix_low = grad_hidden.astype(jnp.bfloat16)
    grad_w_out = jnp.einsum(
        "nd,ne->de", mixed_low, grad_mix_low, preferred_element_type=jnp.float32
    )
    grad_mixed = jnp.einsum(
        "ne,de->nd", grad_mix_low, w_out, preferred_element_type=jnp.float32
    ).reshape(piece_rows, slot_count, model_width)
    grad_query = grad_mixed * filtered
    grad_filtered_low = (grad_mixed * query_conv).astype(jnp.bfloat16)
    grad_piece = lax.all_gather(grad_filtered_low, "seq", axis=0, tiled=True).astype(jnp.float32)
    time_ids = jnp.arange(grad_piece.shape[0], dtype=jnp.int32)
    cos_table, sin_table = wave_tables(freq_ids, time_ids, span_len)
    back_cos = jnp.einsum("ft,tsd->fsd", cos_table, grad_piece, precision=highest)
    back_sin = jnp.einsum("ft,tsd->fsd", sin_table, grad_piece, precision=highest)
    back_cos = back_cos / span_float
    back_sin = back_sin / span_float
    grad_gain_spec = back_cos * sig_cos + back_sin * sig_sin
    grad_sig_cos = spectral_gain * back_cos
    grad_sig_sin = spectral_gain * back_sin
    grad_pre_low = (
        (grad_gain_spec * (1.0 - tanh_value * tanh_value))
        .astype(jnp.bfloat16)
        .reshape(flat_rows, model_width)
    )
    grad_w_cond = jnp.einsum(
        "nc,nd->cd", features_low, grad_pre_low, preferred_element_type=jnp.float32
    )
    grad_cond_bias = jnp.sum(grad_pre_low.astype(jnp.float32), axis=0)
    grad_features = jnp.einsum(
        "nd,cd->nc", grad_pre_low, w_cond, preferred_element_type=jnp.float32
    ).reshape(piece_rows, slot_count, model_width)
    grad_power = grad_features / (1.0 + power_spec)
    grad_cond_cos = 2.0 * cond_cos * grad_power / span_float
    grad_cond_sin = 2.0 * cond_sin * grad_power / span_float
    time_ids = jnp.arange(piece_rows * lax.axis_size("seq"), dtype=jnp.int32)
    cos_table, sin_table = wave_tables(freq_ids, time_ids, span_len)
    signal_term = jnp.einsum(
        "ft,fsd->tsd", cos_table, grad_sig_cos, precision=highest
    ) + jnp.einsum("ft,fsd->tsd", sin_table, grad_sig_sin, precision=highest)
    cond_term = jnp.einsum("ft,fsd->tsd", cos_table, grad_cond_cos, precision=highest) + jnp.einsum(
        "ft,fsd->tsd", sin_table, grad_cond_sin, precision=highest
    )
    source_grads = lax.psum_scatter(
        jnp.concatenate([signal_term, cond_term], axis=2).astype(jnp.bfloat16),
        "seq",
        scatter_dimension=0,
        tiled=True,
    ).astype(jnp.float32)
    grad_signal = source_grads[:, :, :model_width]
    grad_cond = source_grads[:, :, model_width:]
    grad_value_cond, grad_value_rim, grad_cond_taps = conv_backward(
        grad_cond, extended_value, cond_taps, long_flag
    )
    grad_value = grad_signal * key_conv + grad_value_cond
    grad_key = grad_signal * value_f
    value_back = from_behind(grad_value_rim.astype(jnp.bfloat16), "seq", -1).astype(
        grad_value_rim.dtype
    )
    grad_value = jnp.concatenate(
        [grad_value[: piece_rows - 2], grad_value[piece_rows - 2 :] + value_back], axis=0
    )
    grad_conv = jnp.concatenate([grad_query, grad_key, grad_value], axis=2)
    grad_proj_local, grad_proj_rim, grad_short_taps = conv_backward(
        grad_conv, extended_proj, short_taps, long_flag
    )
    proj_back = from_behind(grad_proj_rim.astype(jnp.bfloat16), "seq", -1).astype(
        grad_proj_rim.dtype
    )
    grad_proj = jnp.concatenate(
        [grad_proj_local[: piece_rows - 2], grad_proj_local[piece_rows - 2 :] + proj_back], axis=0
    )
    grad_proj_low = grad_proj.astype(jnp.bfloat16).reshape(flat_rows, 3 * model_width)
    grad_w_in = jnp.einsum(
        "nd,ne->de", normed_one_low, grad_proj_low, preferred_element_type=jnp.float32
    )
    grad_normed_one = jnp.einsum(
        "ne,de->nd", grad_proj_low, w_in, preferred_element_type=jnp.float32
    )
    grad_token_part, grad_ln1 = norm_back(grad_normed_one, unit_one, inv_one, ln1_gain)
    grad_tokens = (grad_hidden + grad_token_part).astype(jnp.bfloat16).reshape(tokens.shape)
    whole_sums = lax.psum(
        (
            grad_ln1,
            grad_w_in,
            grad_short_taps,
            grad_cond_taps,
            grad_w_cond,
            grad_cond_bias,
            grad_w_out,
            grad_ln2,
            grad_gate,
            grad_up,
            grad_down,
        ),
        ("dp", "seq"),
    )
    seq_dims = (0, 0, 1, 1, 0, 0, 0, 0, 0, 0, 0)
    summed = tuple(
        (
            lax.dynamic_slice_in_dim(
                whole_sum,
                seq_rank * (whole_sum.shape[axis_dim] // seq_count),
                whole_sum.shape[axis_dim] // seq_count,
                axis_dim,
            )
            for whole_sum, axis_dim in zip(whole_sums, seq_dims)
        )
    )
    return (
        layer_out,
        grad_tokens,
        summed[0],
        summed[1],
        summed[2],
        summed[3],
        summed[4],
        summed[5],
        summed[6],
        summed[7],
        summed[8],
        summed[9],
        summed[10],
    )


def solution(mesh):
    return jax.shard_map(
        on_device,
        mesh=mesh,
        in_specs=(
            P("dp", "seq", None, None),
            P("dp"),
            P(),
            P(),
            P(),
            P(),
            P(),
            P(),
            P(),
            P(),
            P(),
            P(),
            P(),
            P("dp", "seq", None, None),
        ),
        out_specs=(
            P("dp", "seq", None, None),
            P("dp", "seq", None, None),
            P("seq"),
            P("seq", None),
            P(None, "seq"),
            P(None, "seq"),
            P("seq", None),
            P("seq"),
            P("seq", None),
            P("seq"),
            P("seq", None),
            P("seq", None),
            P("seq", None),
        ),
        check_vma=False,
    )
```

profile of v0, /device:TPU:0, one launch (start us, length us, event | category | flops | bytes accessed | tf_op | source)
XLA Modules:
  0.0 1427.0 jit_solution(9233570854723160421)
XLA Ops:
  12.5 3.9 reshape.284
  19.1 5.5 convolution_convert_fusion
  30.1 5.5 collective-permute-start
  38.7 6.8 reshape.285
  45.5 6.0 copy.77
  63.7 89.3 %all-gather.4.cloned.1.call-done = bf16[512,6,768]{2,0,1:T(8,128)(2,1)} async-done(((bf16[128,6,768]{2,0,1:T(8,128)(2,1)}), bf16[512,6,768]{2,0,1:T(8,128)(2,1)}) %all-gather.4.cloned.1.call-update) | async-done | bytes 4718608 | tf_op jit(solution)/shard_map/all_gather | solution.py:114
  153.0 8.0 fusion.64
  161.0 8.2 log-plus-one_convert_fusion
  175.3 5.0 multiply_subtract_fusion
  183.9 59.2 %all-gather.6.cloned.1.call-done = bf16[512,6,768]{2,0,1:T(8,128)(2,1)} async-done(((bf16[128,6,768]{2,0,1:T(8,128)(2,1)}), bf16[512,6,768]{2,0,1:T(8,128)(2,1)}) %all-gather.6.cloned.1.call-update) | async-done | bytes 4718608 | tf_op jit(solution)/shard_map/all_gather | solution.py:113
  243.1 7.8 fusion.62
  251.0 11.7 fusion.26
  262.7 5.5 fusion.54
  269.6 14.8 %divide_convert_fusion = bf16[512,6,768]{2,0,1:T(8,128)(2,1)} fusion(f32[512,6,768]{2,0,1:T(8,128)S(1)} %fusion.26, f32[]{:T(128)S(6)} %convert_element_type.160, f32[128,6,768]{2,0,1:T(8,128)S(1)} %fusion.54, f32[128,6,768]{2,1,0:T(8,128)S(1)} %copy-done.2, s32[]{:T(128)S(6)} %select_n.103, s32[512]{0:T(512)S(1)} %get-tuple-element.107, ...), kind=kOutput, calls=%fused_computation.8 | convolution fusion | flops 3632332800 | bytes 18879496 | tf_op jit(solution)/shard_map/ft,fsd->tsd/dot_general | solution.py:130
  291.1 77.2 %reduce-scatter.3.cloned.1.call-done = bf16[128,6,768]{2,0,1:T(8,128)(2,1)} async-done(((bf16[512,6,768]{2,0,1:T(8,128)(2,1)}), bf16[128,6,768]{2,0,1:T(8,128)(2,1)}) %reduce-scatter.3.cloned.1.call-update) | async-done | bytes 1179664 | tf_op jit(solution)/shard_map/reduce_scatter | solution.py:133
  380.3 9.2 fusion.142
  389.5 6.2 fusion.143
  395.8 17.3 %multiply_convert_fusion = (bf16[768,3072]{1,0:T(8,128)(2,1)}, bf16[768,3072]{1,0:T(8,128)(2,1)}, bf16[768,3072]{1,0:T(8,128)(2,1)}) fusion(f32[768,3072]{1,0:T(8,128)} %fusion.142, f32[768,3072]{1,0:T(8,128)} %fusion.143, bf16[768,768]{1,0:T(8,128)(2,1)S(1)} %copy-done.31, bf16[3072,768]{1,0:T(8,128)(2,1)} %param.26), kind=kOutput, calls=%fused_computation.3 | convolution fusion | flops 3659268096 | bytes 38928384 | tf_op jit(solution)/shard_map/nd,fd->nf/dot_general | solution.py:149
  413.1 7.7 fusion.144
  420.9 7.3 multiply_reduce_fusion.2
  436.8 5.7 convert_multiply_fusion
  446.3 86.3 %all-gather.8.cloned.1.call-done = bf16[512,6,768]{2,0,1:T(8,128)(2,1)} async-done(((bf16[128,6,768]{2,0,1:T(8,128)(2,1)}), bf16[512,6,768]{2,0,1:T(8,128)(2,1)}) %all-gather.8.cloned.1.call-update) | async-done | bytes 4718608 | tf_op jit(solution)/shard_map/all_gather | solution.py:174
  532.6 7.9 convolution_divide_fusion.1
  540.6 11.6 fusion.23
  552.3 9.2 convert_reduce_fusion
  561.5 4.3 add_divide_fusion.1
  565.7 11.2 fusion.18
  577.0 15.4 %add_convert_fusion = bf16[512,6,768]{2,0,1:T(8,128)(2,1)} fusion(f32[512,6,768]{2,0,1:T(8,128)S(1)} %fusion.18, f32[128,6,768]{2,0,1:T(8,128)S(1)} %add_divide_fusion.1, f32[128,6,768]{2,0,1:T(8,128)} %get-tuple-element.101, f32[]{:T(128)S(6)} %convert_element_type.160, s32[]{:T(128)S(6)} %select_n.103, s32[512]{0:T(512)S(1)} %get-tuple-element.107, ...), kind=kOutput, calls=%fused_computation.1 | convolution fusion | flops 3631153152 | bytes 18879496 | tf_op jit(solution)/shard_map/ft,fsd->tsd/dot_general | solution.py:204
  592.3 15.3 %add_convert_fusion.1 = bf16[512,6,768]{2,0,1:T(8,128)(2,1)S(1)} fusion(f32[512,6,768]{2,0,1:T(8,128)S(1)} %fusion.23, f32[128,6,768]{2,0,1:T(8,128)} %get-tuple-element.105, f32[128,6,768]{2,1,0:T(8,128)S(1)} %copy-done.3, f32[]{:T(128)S(6)} %convert_element_type.160, s32[]{:T(128)S(6)} %select_n.103, s32[512]{0:T(512)S(1)} %get-tuple-element.107, ...), kind=kOutput, calls=%fused_computation.2 | convolution fusion | flops 3629973504 | bytes 18879496 | tf_op jit(solution)/shard_map/ft,fsd->tsd/dot_general | solution.py:203
  607.6 4.4 pad_maximum_fusion
  619.9 4.7 fusion.41
  624.6 8.8 fusion.146
  633.5 6.3 fusion.147
  639.8 6.3 fusion.148
  648.8 123.1 %reduce-scatter.5.cloned.1.call-done = bf16[128,6,1536]{2,0,1:T(8,128)(2,1)} async-done(((bf16[512,6,1536]{2,0,1:T(8,128)(2,1)}), bf16[128,6,1536]{2,0,1:T(8,128)(2,1)}) %reduce-scatter.5.cloned.1.call-update) | async-done | bytes 2359312 | tf_op jit(solution)/shard_map/reduce_scatter | solution.py:207
  776.2 4.2 multiply_reduce_fusion.4
  780.8 4.6 multiply_reduce_fusion.1
  792.7 4.1 copy.96
  796.8 6.6 convert_element_type.184
  803.4 8.2 fusion.145
  811.7 4.9 copy.98
  816.6 10.0 add_convert_fusion.3
  832.5 4.1 concatenate.42
  836.5 4.8 copy.99
  841.3 3.9 concatenate.43
  858.6 4.9 fusion.6
  876.4 44.4 %all-reduce.2 = (f32[768]{0:T(1024)}, f32[3,2304]{1,0:T(4,128)}, f32[3,768]{1,0:T(4,128)}, f32[768]{0:T(1024)}, f32[768]{0:T(1024)}) all-reduce(f32[768]{0:T(1024)} %get-tuple-element.58, f32[3,2304]{1,0:T(4,128)} %pad_maximum_fusion.4, f32[3,768]{1,0:T(4,128)S(1)} %copy-done.56, ...), channel_id=1, replica_groups=mesh['dp'=8,'seq'=4] {'dp','seq'}, use_global_device_ids=true, to_apply=%region_11.12 | all-reduce | flops 11520 | bytes 92160 | tf_op jit(solution)/shard_map/psum | solution.py:245
  927.5 476.0 %all-reduce.6.cloned.1.call-done = (f32[768,2304]{1,0:T(8,128)}, f32[768,768]{1,0:T(8,128)}, f32[768,768]{1,0:T(8,128)}, f32[768,3072]{1,0:T(8,128)}, f32[768,3072]{1,0:T(8,128)}, /*index=5*/f32[3072,768]{1,0:T(8,128)}) async-done(((f32[768,2304]{1,0:T(8,128)}, f32[768,768]{1,0:T(8,128)}, f32[768,768]{1,0:T(8,128)}, f32[768,3072]{1,0:T(8,128)}, f32[768,3072]{1,0:T(8,128)}, ...) | async-done | bytes 40108048 | tf_op jit(solution)/shard_map/psum | solution.py:245
  (277 shorter events, 147.6 us)
Async XLA Ops:
  7.2 11.9 copy-start
  7.2 145.8 %all-gather.4.cloned.1.call-start = ((), (), s32[]{:S(2)}) async-start(), calls=%async_computation.2 | async-start | bytes 5898240 | tf_op jit(solution)/shard_map/all_gather | solution.py:114
  12.5 6.6 copy-start.63
  16.4 8.2 copy-start.57
  18.1 6.5 copy-start.65
  30.1 22.0 %collective-permute-start = (bf16[2,6,2304]{2,0,1:T(2,128)(2,1)}, bf16[2,6,2304]{2,0,1:T(2,128)(2,1)}, u32[]{:S(2)}, u32[]{:S(2)}) collective-permute-start(bf16[2,6,2304]{2,0,1:T(2,128)(2,1)} %copy.78), channel_id=1, source_target_pairs={{0,1},{1,2},{2,3},{4,5},{5,6},{6,7},{8,9},{9,10},{10,11},{12,13},{... | collective-permute-start | bytes 165896 | tf_op jit(solution)/shard_map/ppermute | solution.py:14
  37.2 15.8 %copy-start.44 = (f32[2304]{0:T(1024)}, f32[2304]{0:T(1024)S(1)}, u32[]{:S(2)}) copy-start(f32[2304]{0:T(1024)S(1)} %get-tuple-element.64) | copy-start | bytes 27652
  38.7 21.7 %copy-start.52 = (f32[768]{0:T(1024)}, f32[768]{0:T(1024)S(1)}, u32[]{:S(2)}) copy-start(f32[768]{0:T(1024)S(1)} %get-tuple-element.67) | copy-start | bytes 9220
  45.5 7.6 copy-start.46
  45.5 7.6 copy-start.48
  55.8 6.7 copy-start.4
  55.9 4.5 collective-permute-start.1
  62.5 180.6 %all-gather.6.cloned.1.call-start = ((), (), s32[]{:S(2)}) async-start(), calls=%async_computation.3 | async-start | bytes 5898240 | tf_op jit(solution)/shard_map/all_gather | solution.py:113
  63.2 305.1 %reduce-scatter.3.cloned.1.call-start = ((), (), s32[]{:S(2)}) async-start(), calls=%async_computation.4 | async-start | bytes 5898240 | tf_op jit(solution)/shard_map/reduce_scatter | solution.py:133
  153.0 8.0 copy-start.33
  161.0 8.2 copy-start.27
  243.1 7.8 copy-start.2
  243.1 19.6 %slice-start.2 = ((s8[4718592]{0:T(1024)(128)(4,1)}), s8[4194304]{0:T(1024)(128)(4,1)S(1)}, s32[]{:S(2)}) async-start(s8[4718592]{0:T(1024)(128)(4,1)} %bitcast.76), calls=%async_computation.10 | async-start | bytes 8388608
  251.0 11.7 copy-start.7
  251.0 11.7 slice-start.3
  284.5 248.1 %all-gather.8.cloned.1.call-start = ((), (), s32[]{:S(2)}) async-start(), calls=%async_computation.5 | async-start | bytes 5898240 | tf_op jit(solution)/shard_map/all_gather | solution.py:174
  379.2 49.0 %copy-start.5 = (f32[768,768]{1,0:T(8,128)}, f32[768,768]{1,0:T(8,128)S(1)}, u32[]{:S(2)}) copy-start(f32[768,768]{1,0:T(8,128)S(1)} %get-tuple-element.103) | copy-start | bytes 7077892
  379.9 9.6 slice-start.8
  380.2 9.3 copy-start.22
  380.3 9.3 slice-start.9
  389.5 6.3 copy-start.31
  413.1 7.8 copy-start.34
  442.5 329.4 %reduce-scatter.5.cloned.1.call-start = ((), (), s32[]{:S(2)}) async-start(), calls=%async_computation.6 | async-start | bytes 11796480 | tf_op jit(solution)/shard_map/reduce_scatter | solution.py:207
  532.6 8.0 copy-start.3
  532.6 19.6 %slice-start.4 = ((s8[4718592]{0:T(1024)(128)(4,1)}), s8[4194304]{0:T(1024)(128)(4,1)S(1)}, s32[]{:S(2)}) async-start(s8[4718592]{0:T(1024)(128)(4,1)} %bitcast.78), calls=%async_computation.12 | async-start | bytes 8388608
  540.5 11.7 copy-start.8
  540.6 11.7 copy-start.24
  540.6 11.7 copy-start.26
  540.6 11.7 slice-start.5
  552.3 9.2 copy-start.28
  592.3 15.3 %copy-start.18 = (bf16[512,6,768]{2,0,1:T(8,128)(2,1)S(1)}, bf16[512,6,768]{2,0,1:T(8,128)(2,1)}, u32[]{:S(2)}) copy-start(bf16[512,6,768]{2,0,1:T(8,128)(2,1)} %add_convert_fusion) | copy-start | bytes 14155780
  612.0 791.5 %all-reduce.6.cloned.1.call-start = ((), (), s32[]{:S(2)}) async-start(), calls=%async_computation.7 | async-start | bytes 80216064 | tf_op jit(solution)/shard_map/psum | solution.py:245
  619.9 13.5 slice-start.6
  624.6 8.8 slice-start.7
  624.6 15.2 %slice-start.10 = ((s8[4718592]{0:T(1024)(128)(4,1)}), s8[4194304]{0:T(1024)(128)(4,1)S(1)}, s32[]{:S(2)}) async-start(s8[4718592]{0:T(1024)(128)(4,1)} %bitcast.84), calls=%async_computation.18 | async-start | bytes 8388608
  633.5 6.3 copy-start.32
  633.5 6.3 slice-start.11
  639.8 6.4 copy-start.36
  639.8 6.4 copy-start.38
  648.8 125.6 %copy-start.53 = (f32[768]{0:T(1024)S(1)}, f32[768]{0:T(1024)}, u32[]{:S(2)}) copy-start(f32[768]{0:T(1024)} %copy-done.52) | copy-start | bytes 9220
  648.8 125.6 %copy-start.55 = (f32[768]{0:T(1024)S(1)}, f32[768]{0:T(1024)}, u32[]{:S(2)}) copy-start(f32[768]{0:T(1024)} %get-tuple-element.68) | copy-start | bytes 9220
  774.5 5.9 collective-permute-start.2
  785.6 6.8 collective-permute-start.3
  (45 other events, 172.8 us)
Sparse Core Ops, SparseCore 0:
  62.6 90.3 all-gather.3
  155.2 87.9 all-gather.5
  284.6 83.6 reduce-scatter.2
  442.6 89.9 all-gather.7
  612.1 159.7 reduce-scatter.4
  811.8 591.6 all-reduce.5
where the time goes:
time: 1440 us; the launch traced here: 1430 us
  waiting for transfers between devices  916 us (64%)
  matrix products  246 us (17%)
  local copies, waits for them, and re-layouts  146 us (10%)
  other arithmetic  46.6 us (3%)
  blocking collectives  44.4 us (3%)
  between operations  16.2 us (1%)
    psum x1, waiting for transfers between devices, on_device(): lax.psum((grad_ln1, grad_w_in, grad_short_taps, grad_cond_taps, grad_w_co...  476 us
    reduce_scatter x1, waiting for transfers between devices, on_device(): lax.psum_scatter(jnp.concatenate([signal_term, cond_term], axis=2).astype...  123 us
    all_gather x1, waiting for transfers between devices, on_device(): lax.all_gather(cond_low, 'seq', axis=0, tiled=True).astype(jnp.float32)  89.3 us
    all_gather x1, waiting for transfers between devices, on_device(): lax.all_gather(grad_filtered_low, 'seq', axis=0, tiled=True)  86.3 us
    reduce_scatter x1, waiting for transfers between devices, on_device(): lax.psum_scatter((term / span_float).astype(jnp.bfloat16), 'seq', scatter...  77.2 us
    all_gather x1, waiting for transfers between devices, on_device(): lax.all_gather(signal_low, 'seq', axis=0, tiled=True).astype(jnp.float32)  59.2 us
    psum x1, blocking collectives, on_device(): lax.psum((grad_ln1, grad_w_in, grad_short_taps, grad_cond_taps, grad_w_co...  44.4 us
  transfers between devices with their start and end apart: 10, of which 8 were waited for; matrix products, arithmetic and copies ran while one was open for 12% of the time, Pallas kernels for 0%

commit v1 on v0

--- a/solution.py
+++ b/solution.py
@@ -242,7 +242,7 @@
     )
     grad_token_part, grad_ln1 = norm_back(grad_normed_one, unit_one, inv_one, ln1_gain)
     grad_tokens = (grad_hidden + grad_token_part).astype(jnp.bfloat16).reshape(tokens.shape)
-    whole_sums = lax.psum(
+    partial = lax.psum(
         (
             grad_ln1,
             grad_w_in,
@@ -256,8 +256,9 @@
             grad_up,
             grad_down,
         ),
-        ("dp", "seq"),
-    )
+        "seq",
+    )
+    whole_sums = lax.psum(partial, "dp")
     seq_dims = (0, 0, 1, 1, 0, 0, 0, 0, 0, 0, 0)
     summed = tuple(
         (

time: 1440 us -> 2650 us (1.84)
  waiting for transfers between devices: 916 us -> 2130 us
    psum x1, waiting for transfers between devices: 476 us -> 1330 us  [on_device(): lax.psum((grad_ln1, grad_w_in, grad_short_taps, grad_cond_taps, grad_w_co...]
    psum x0 -> x1, waiting for transfers between devices: none -> 364 us  [on_device(): whole_sums = lax.psum(partial, 'dp')]
  transfers between devices with their start and end apart: 10 -> 11, of which waited for: 8 -> 9; matrix products, arithmetic and copies ran while one was open for 12% -> 6% of each run, Pallas kernels for 0% -> 0%
where the time goes in v1:
time: 2650 us; the launch traced here: 2640 us
  waiting for transfers between devices  2130 us (80%)
  matrix products  245 us (9%)
  local copies, waits for them, and re-layouts  145 us (5%)
  other arithmetic  46.5 us (2%)
  blocking collectives  45.2 us (2%)
    psum x1, waiting for transfers between devices, on_device(): lax.psum((grad_ln1, grad_w_in, grad_short_taps, grad_cond_taps, grad_w_co...  1330 us
    psum x1, waiting for transfers between devices, on_device(): whole_sums = lax.psum(partial, 'dp')  364 us
    reduce_scatter x1, waiting for transfers between devices, on_device(): lax.psum_scatter(jnp.concatenate([signal_term, cond_term], axis=2).astype...  123 us
    all_gather x1, waiting for transfers between devices, on_device(): lax.all_gather(cond_low, 'seq', axis=0, tiled=True).astype(jnp.float32)  89.3 us
    all_gather x1, waiting for transfers between devices, on_device(): lax.all_gather(grad_filtered_low, 'seq', axis=0, tiled=True)  86.2 us
    reduce_scatter x1, waiting for transfers between devices, on_device(): lax.psum_scatter((term / span_float).astype(jnp.bfloat16), 'seq', scatter...  77.2 us
    all_gather x1, waiting for transfers between devices, on_device(): lax.all_gather(signal_low, 'seq', axis=0, tiled=True).astype(jnp.float32)  59.2 us
  transfers between devices with their start and end apart: 11, of which 9 were waited for; matrix products, arithmetic and copies ran while one was open for 6% of the time, Pallas kernels for 0%

profile of v1, /device:TPU:0, one launch (start us, length us, event | category | flops | bytes accessed | tf_op | source)
XLA Modules:
  0.0 2639.4 jit_solution(13894792493976377782)
XLA Ops:
  19.1 5.5 convolution_convert_fusion
  30.1 5.5 collective-permute-start
  38.7 6.8 reshape.285
  45.5 6.0 copy.77
  63.7 89.3 %all-gather.4.cloned.1.call-done = bf16[512,6,768]{2,0,1:T(8,128)(2,1)} async-done(((bf16[128,6,768]{2,0,1:T(8,128)(2,1)}), bf16[512,6,768]{2,0,1:T(8,128)(2,1)}) %all-gather.4.cloned.1.call-update) | async-done | bytes 4718608 | tf_op jit(solution)/shard_map/all_gather | solution.py:114
  153.0 8.0 fusion.64
  161.0 8.2 log-plus-one_convert_fusion
  175.3 5.0 multiply_subtract_fusion
  183.9 59.2 %all-gather.6.cloned.1.call-done = bf16[512,6,768]{2,0,1:T(8,128)(2,1)} async-done(((bf16[128,6,768]{2,0,1:T(8,128)(2,1)}), bf16[512,6,768]{2,0,1:T(8,128)(2,1)}) %all-gather.6.cloned.1.call-update) | async-done | bytes 4718608 | tf_op jit(solution)/shard_map/all_gather | solution.py:113
  243.1 7.8 fusion.62
  251.0 11.7 fusion.26
  262.7 5.5 fusion.54
  269.6 14.8 divide_convert_fusion
  291.1 77.2 %reduce-scatter.3.cloned.1.call-done = bf16[128,6,768]{2,0,1:T(8,128)(2,1)} async-done(((bf16[512,6,768]{2,0,1:T(8,128)(2,1)}), bf16[128,6,768]{2,0,1:T(8,128)(2,1)}) %reduce-scatter.3.cloned.1.call-update) | async-done | bytes 1179664 | tf_op jit(solution)/shard_map/reduce_scatter | solution.py:133
  380.2 9.2 fusion.142
  389.5 6.2 fusion.143
  395.7 17.2 multiply_convert_fusion
  413.0 7.7 fusion.144
  420.7 7.3 multiply_reduce_fusion.2
  436.7 5.7 convert_multiply_fusion
  446.2 86.2 %all-gather.8.cloned.1.call-done = bf16[512,6,768]{2,0,1:T(8,128)(2,1)} async-done(((bf16[128,6,768]{2,0,1:T(8,128)(2,1)}), bf16[512,6,768]{2,0,1:T(8,128)(2,1)}) %all-gather.8.cloned.1.call-update) | async-done | bytes 4718608 | tf_op jit(solution)/shard_map/all_gather | solution.py:174
  532.5 7.9 convolution_divide_fusion.1
  540.5 11.6 fusion.23
  552.2 9.2 convert_reduce_fusion
  561.4 4.3 add_divide_fusion.1
  565.7 11.2 fusion.18
  576.9 15.4 add_convert_fusion
  592.3 15.3 add_convert_fusion.1
  607.6 4.4 pad_maximum_fusion
  619.9 4.7 fusion.41
  624.7 8.9 fusion.146
  633.6 6.3 fusion.147
  639.9 6.3 fusion.148
  648.8 123.1 %reduce-scatter.5.cloned.1.call-done = bf16[128,6,1536]{2,0,1:T(8,128)(2,1)} async-done(((bf16[512,6,1536]{2,0,1:T(8,128)(2,1)}), bf16[128,6,1536]{2,0,1:T(8,128)(2,1)}) %reduce-scatter.5.cloned.1.call-update) | async-done | bytes 2359312 | tf_op jit(solution)/shard_map/reduce_scatter | solution.py:207
  776.2 4.2 multiply_reduce_fusion.4
  780.8 4.6 multiply_reduce_fusion.1
  792.7 4.1 copy.96
  796.8 6.6 convert_element_type.184
  803.4 8.2 fusion.145
  811.6 1326.3 %all-reduce.11.cloned.1.call-done = (f32[768,2304]{1,0:T(8,128)}, f32[768,768]{1,0:T(8,128)}, f32[768,768]{1,0:T(8,128)}, f32[768,3072]{1,0:T(8,128)}, f32[768,3072]{1,0:T(8,128)}, /*index=5*/f32[3072,768]{1,0:T(8,128)}) async-done(((f32[768,2304]{1,0:T(8,128)}, f32[768,768]{1,0:T(8,128)}, f32[768,768]{1,0:T(8,128)}, f32[768,3072]{1,0:T(8,128)}, f32[768,3072]{1,0:T(8,128)}, ...) | async-done | bytes 40108048 | tf_op jit(solution)/shard_map/psum | solution.py:245
  2138.0 4.9 copy.98
  2142.9 8.6 add_convert_fusion.3
  2157.5 4.0 concatenate.42
  2161.5 4.7 copy.99
  2183.6 4.8 fusion.6
  2201.3 19.4 all-reduce.4
  2220.7 25.9 all-reduce.2
  2251.9 364.0 %all-reduce.9.cloned.1.call-done = (f32[768,2304]{1,0:T(8,128)}, f32[768,768]{1,0:T(8,128)}, f32[768,768]{1,0:T(8,128)}, f32[768,3072]{1,0:T(8,128)}, f32[768,3072]{1,0:T(8,128)}, /*index=5*/f32[3072,768]{1,0:T(8,128)}) async-done(((f32[768,2304]{1,0:T(8,128)}, f32[768,768]{1,0:T(8,128)}, f32[768,768]{1,0:T(8,128)}, f32[768,3072]{1,0:T(8,128)}, f32[768,3072]{1,0:T(8,128)}, ...) | async-done | bytes 40108048 | tf_op jit(solution)/shard_map/psum | solution.py:261
  (281 shorter events, 154.3 us)
Async XLA Ops:
  7.2 11.9 copy-start
  7.2 145.8 %all-gather.4.cloned.1.call-start = ((), (), s32[]{:S(2)}) async-start(), calls=%async_computation.2 | async-start | bytes 5898240 | tf_op jit(solution)/shard_map/all_gather | solution.py:114
  12.5 6.6 copy-start.63
  16.4 8.2 copy-start.57
  18.1 6.5 copy-start.65
  30.1 22.0 collective-permute-start
  37.2 15.8 copy-start.44
  38.7 21.7 copy-start.52
  45.5 7.6 copy-start.46
  45.5 7.6 copy-start.48
  55.8 6.7 copy-start.4
  55.9 4.5 collective-permute-start.1
  62.5 180.6 %all-gather.6.cloned.1.call-start = ((), (), s32[]{:S(2)}) async-start(), calls=%async_computation.3 | async-start | bytes 5898240 | tf_op jit(solution)/shard_map/all_gather | solution.py:113
  63.2 305.0 %reduce-scatter.3.cloned.1.call-start = ((), (), s32[]{:S(2)}) async-start(), calls=%async_computation.4 | async-start | bytes 5898240 | tf_op jit(solution)/shard_map/reduce_scatter | solution.py:133
  153.0 8.0 copy-start.33
  161.0 8.2 copy-start.27
  243.1 7.8 copy-start.2
  243.1 19.6 slice-start.2
  251.0 11.7 copy-start.7
  251.0 11.7 slice-start.3
  284.4 248.1 %all-gather.8.cloned.1.call-start = ((), (), s32[]{:S(2)}) async-start(), calls=%async_computation.5 | async-start | bytes 5898240 | tf_op jit(solution)/shard_map/all_gather | solution.py:174
  379.1 48.9 %copy-start.5 = (f32[768,768]{1,0:T(8,128)}, f32[768,768]{1,0:T(8,128)S(1)}, u32[]{:S(2)}) copy-start(f32[768,768]{1,0:T(8,128)S(1)} %get-tuple-element.114) | copy-start | bytes 7077892
  379.8 9.6 slice-start.8
  380.2 9.3 copy-start.22
  380.2 9.3 slice-start.9
  413.0 7.8 copy-start.34
  442.4 329.5 %reduce-scatter.5.cloned.1.call-start = ((), (), s32[]{:S(2)}) async-start(), calls=%async_computation.6 | async-start | bytes 11796480 | tf_op jit(solution)/shard_map/reduce_scatter | solution.py:207
  532.5 8.0 copy-start.3
  532.5 19.6 slice-start.4
  540.5 11.7 copy-start.8
  540.5 11.7 copy-start.24
  540.5 11.7 copy-start.26
  540.5 11.7 slice-start.5
  552.2 9.2 copy-start.28
  592.3 15.3 copy-start.18
  612.0 1525.9 %all-reduce.11.cloned.1.call-start = ((), (), s32[]{:S(2)}) async-start(), calls=%async_computation.8 | async-start | bytes 80216064 | tf_op jit(solution)/shard_map/psum | solution.py:245
  619.9 13.7 slice-start.6
  624.6 8.9 slice-start.7
  624.6 15.2 slice-start.10
  633.6 6.3 copy-start.32
  633.6 6.3 slice-start.11
  639.9 6.4 copy-start.36
  639.9 6.4 copy-start.38
  648.8 125.6 %copy-start.53 = (f32[768]{0:T(1024)S(1)}, f32[768]{0:T(1024)}, u32[]{:S(2)}) copy-start(f32[768]{0:T(1024)} %copy-done.52) | copy-start | bytes 9220
  648.8 125.6 %copy-start.55 = (f32[768]{0:T(1024)S(1)}, f32[768]{0:T(1024)}, u32[]{:S(2)}) copy-start(f32[768]{0:T(1024)} %get-tuple-element.68) | copy-start | bytes 9220
  774.5 5.9 collective-permute-start.2
  785.6 6.8 collective-permute-start.3
  811.6 1804.3 %all-reduce.9.cloned.1.call-start = ((), (), s32[]{:S(2)}) async-start(), calls=%async_computation.7 | async-start | bytes 80216064 | tf_op jit(solution)/shard_map/psum | solution.py:261
  (46 other events, 178.3 us)
Sparse Core Ops, SparseCore 0:
  62.6 90.3 all-gather.3
  155.2 87.9 all-gather.5
  284.5 83.6 reduce-scatter.2
  442.5 89.9 all-gather.7
  612.1 159.7 reduce-scatter.4
  811.7 1326.1 all-reduce.10
  2142.9 472.9 all-reduce.8
